TPU v7x, 32 devices: a whole 2x2x4 slice. The times are simulated.
32 devices in a mesh: row: 4 (over y, x), col: 8 (over z, core).
Axes of the slice: x: 2, y: 2, z: 4, core: 2. Of those that a mesh axis runs over, the one named last changes fastest.
Arguments:
- anc_inverse: float32 [10240, 10240], P('row', 'col'), may hold values from -0.0625 to 0.0625
- lower_anc: float32 [10240, 3, 384], P('col', None, 'row'), may hold values from -1.5 to 1.5
- upper_anc: float32 [10240, 3, 384], P('row', None, 'col'), may hold values from -0.75 to 0.75
- lower_edge: float32 [2, 384, 384], replicated, may hold values from -0.3125 to 0.3125
- upper_edge: float32 [2, 384, 384], replicated, may hold values from -0.3125 to 0.3125
- diag_inverse: float32 [3, 384, 384], replicated, may hold values from -6 to 6
- tile_mask: int32 [3, 80, 3], replicated, may hold values 0 or 1
Outputs:
- x_blocks: float32 [10240, 3, 384], P(('row', 'col'))
- y_blocks: float32 [8, 4, 320, 3, 384], P('col', 'row')
- z_blocks: float32 [3, 384, 384], P(None, 'row', 'col')
- cross_blocks: float32 [2, 2, 384, 384], P(None, None, 'row', 'col')
All inputs are finite; a program needn't handle non-finite values.
Results may differ from a plain program's by a relative error of at most 0.0001.
Values sent between devices are 32-bit elements; how exact they have to be, the bound alone decides.
A program may use at most 128 MiB of HBM per device.

v0:
```python
import jax
import jax.numpy as jnp
from jax import lax
from jax.sharding import PartitionSpec as P

W = 384
BLK = 128
SUPER = 3
precise = lax.Precision.HIGHEST


def product(left, right):
    return jnp.dot(left, right, precision=precise, preferred_element_type=jnp.float32)


def inner_product(left, right):
    return lax.dot_general(
        left, right, (((0,), (0,)), ((), ())), precision=precise, preferred_element_type=jnp.float32
    )


def outer_product(left, right):
    return lax.dot_general(
        left, right, (((1,), (1,)), ((), ())), precision=precise, preferred_element_type=jnp.float32
    )


def tile_pattern(tile_mask, first_block, blocks):
    window = lax.dynamic_slice_in_dim(tile_mask, first_block, blocks, 1).astype(jnp.float32)
    window = jnp.transpose(window, (1, 0, 2))
    widened = jnp.broadcast_to(window[:, None, :, :, None], (blocks, BLK, SUPER, W // BLK, BLK))
    return widened.reshape(blocks * BLK, SUPER, W)


def row_term(anc_inverse, lower_cols):
    return product(anc_inverse, lower_cols)


def col_term(anc_inverse, upper_rows):
    return inner_product(anc_inverse, upper_rows)


def per_device(anc_inverse, lower_anc, upper_anc, lower_edge, upper_edge, diag_inverse, tile_mask):
    rows_here, cols_here = anc_inverse.shape
    slab_rows = rows_here // lax.axis_size("col")
    row_index = lax.axis_index("row")
    col_index = lax.axis_index("col")
    col_pattern = tile_pattern(tile_mask, col_index * (cols_here // BLK), cols_here // BLK)
    row_pattern = tile_pattern(tile_mask, row_index * (rows_here // BLK), rows_here // BLK)
    lower_list = []
    upper_list = []
    cols_list = []
    rows_list = []
    lower_full = lax.all_gather(lower_anc, "row", axis=2, tiled=True) * col_pattern
    upper_full = lax.all_gather(upper_anc, "col", axis=2, tiled=True) * row_pattern
    cols_all = lax.psum_scatter(
        row_term(anc_inverse, lower_full.reshape(cols_here, SUPER * W)),
        "col",
        scatter_dimension=0,
        tiled=True,
    )
    rows_all = lax.psum_scatter(
        col_term(anc_inverse, upper_full.reshape(rows_here, SUPER * W)),
        "row",
        scatter_dimension=0,
        tiled=True,
    )
    cols_all = cols_all.reshape(slab_rows, SUPER, W)
    rows_all = rows_all.reshape(slab_rows, SUPER, W)
    for node_index in range(SUPER):
        lower_list.append(lower_full[:, node_index, :])
        upper_list.append(upper_full[:, node_index, :])
        cols_list.append(cols_all[:, node_index, :])
        rows_list.append(rows_all[:, node_index, :])
    x_list = []
    y_list = []
    corner_list = []
    cross_cols = []
    cross_rows = []
    for node_index in range(SUPER):
        lower_cur = lower_list[node_index]
        upper_cur = upper_list[node_index]
        inv_cols = -cols_list[node_index]
        inv_rows = -rows_list[node_index]
        upper_mine = lax.dynamic_slice_in_dim(upper_cur, col_index * slab_rows, slab_rows, 0)
        if node_index > 0:
            lower_side = lower_edge[node_index - 1]
            upper_side = upper_edge[node_index - 1]
            lower_mine = lax.dynamic_slice_in_dim(lower_cur, row_index * slab_rows, slab_rows, 0)
            rows_lower = inner_product(prev_rows, lower_mine)
            upper_cols = inner_product(upper_mine, prev_cols)
        if node_index > 0:
            rows_lower, upper_cols = lax.psum((rows_lower, upper_cols), ("row", "col"))
        if node_index > 0:
            cross_col = -(rows_lower + product(prev_corner, lower_side))
            cross_row = -(upper_cols + product(upper_side, prev_corner))
            inv_cols = inv_cols - product(prev_cols, lower_side)
            inv_rows = inv_rows - outer_product(prev_rows, upper_side)
            cross_cols.append(cross_col)
            cross_rows.append(cross_row)
        inv_corner = diag_inverse[node_index] - lax.psum(
            inner_product(upper_mine, inv_cols), ("row", "col")
        )
        if node_index > 0:
            inv_corner = inv_corner - product(upper_side, cross_col)
        x_list.append(inv_cols)
        y_list.append(inv_rows)
        corner_list.append(inv_corner)
        prev_cols = inv_cols
        prev_rows = inv_rows
        prev_corner = inv_corner
    x_blocks = jnp.stack(x_list, axis=1)
    y_blocks = jnp.stack(y_list, axis=1)[None, None]
    tile_rows = W // lax.axis_size("row")
    tile_cols = W // lax.axis_size("col")
    corners = jnp.stack(corner_list)
    corners = lax.dynamic_slice_in_dim(corners, row_index * tile_rows, tile_rows, 1)
    z_blocks = lax.dynamic_slice_in_dim(corners, col_index * tile_cols, tile_cols, 2)
    crossed = jnp.stack([jnp.stack(cross_cols), jnp.stack(cross_rows)])
    crossed = lax.dynamic_slice_in_dim(crossed, row_index * tile_rows, tile_rows, 2)
    cross_blocks = lax.dynamic_slice_in_dim(crossed, col_index * tile_cols, tile_cols, 3)
    return (x_blocks, y_blocks, z_blocks, cross_blocks)


def solution(mesh):
    return jax.shard_map(
        per_device,
        mesh=mesh,
        in_specs=(
            P("row", "col"),
            P("col", None, "row"),
            P("row", None, "col"),
            P(),
            P(),
            P(),
            P(),
        ),
        out_specs=(
            P(("row", "col"), None, None),
            P("col", "row", None, None, None),
            P(None, "row", "col"),
            P(None, None, "row", "col"),
        ),
        check_vma=False,
    )
```

profile of v0, /device:TPU:0, one launch (start us, length us, event | category | flops | bytes accessed | tf_op | source)
XLA Modules:
  0.0 565.6 jit_solution(17613502817447202190)
XLA Ops:
  8.9 4.2 broadcast_in_dim.6
  13.1 10.5 %reshape.42 = f32[1280,3,384]{2,0,1:T(8,128)} reshape(f32[10,128,3,3,128]{4,3,1,0,2:T(4,128)} %broadcast_in_dim.6) | data formatting | bytes 11796480 | tf_op jit(solution)/shard_map/reshape | solution.py:32
  23.6 55.8 %all-gather.3.cloned.1.call-done = f32[1280,3,384]{0,2,1:T(8,128)} async-done(((f32[1280,3,96]{0,2,1:T(8,128)}), f32[1280,3,384]{0,2,1:T(8,128)}) %all-gather.3.cloned.1.call-update) | async-done | bytes 5898256 | tf_op jit(solution)/shard_map/all_gather | solution.py:54
  79.3 7.7 %copy.70 = f32[1280,3,384]{2,0,1:T(8,128)} copy(f32[1280,3,384]{0,2,1:T(8,128)} %all-gather.3.cloned.1.call-done) | data formatting | bytes 11796480 | tf_op jit(solution)/shard_map/all_gather | solution.py:54
  87.0 9.3 %mul.30 = f32[1280,3,384]{2,0,1:T(8,128)} multiply(f32[1280,3,384]{2,0,1:T(8,128)} %copy.70, f32[1280,3,384]{2,0,1:T(8,128)} %reshape.42) | non-fusion elementwise | flops 1474560 | bytes 17694720 | tf_op jit(solution)/shard_map/mul | solution.py:54
  96.3 7.8 %copy.71 = f32[1280,3,384]{0,2,1:T(8,128)} copy(f32[1280,3,384]{2,0,1:T(8,128)} %mul.30) | data formatting | bytes 11796480 | tf_op jit(solution)/shard_map/mul | solution.py:54
  104.0 52.7 %convolution_bitcast_fusion = f32[2560,1152]{0,1:T(8,128)} fusion(f32[1280,1152]{0,1:T(8,128)} %bitcast.163, f32[2560,1280]{1,0:T(8,128)} %param.7), kind=kOutput, calls=%fused_computation | convolution fusion | flops 45298483200 | bytes 30801920 | tf_op jit(solution)/shard_map/dot_general | solution.py:13
  156.8 13.6 %copy.92 = f32[2560,1152]{1,0:T(8,128)} copy(f32[2560,1152]{0,1:T(8,128)} %convolution_bitcast_fusion) | data formatting | bytes 23592960
  171.1 6.0 %broadcast_in_dim.7 = f32[20,128,3,3,128]{1,0,4,3,2:T(8,128)} broadcast(f32[20,3,3]{0,2,1:T(4,128)S(1)} %convert_bitcast_fusion), dimensions={0,2,3} | broadcast | bytes 11797200 | tf_op jit(solution)/shard_map/broadcast_in_dim | solution.py:31
  177.1 13.7 %reshape.45 = f32[2560,3,384]{0,2,1:T(8,128)} reshape(f32[20,128,3,3,128]{1,0,4,3,2:T(8,128)} %broadcast_in_dim.7) | data formatting | bytes 23592960 | tf_op jit(solution)/shard_map/reshape | solution.py:32
  191.2 9.7 %mul.32 = f32[2560,3,384]{0,2,1:T(8,128)S(1)} multiply(f32[2560,3,384]{0,2,1:T(8,128)} %all-gather.5.cloned.1.call-done, f32[2560,3,384]{0,2,1:T(8,128)} %reshape.45) | non-fusion elementwise | flops 2949120 | bytes 35389440 | tf_op jit(solution)/shard_map/mul | solution.py:55
  200.9 4.3 copy-done
  205.3 50.1 %convolution_bitcast_fusion.1 = f32[1280,1152]{0,1:T(8,128)} fusion(f32[2560,1152]{0,1:T(8,128)S(1)} %bitcast.157, f32[2560,1280]{1,0:T(8,128)} %param.7), kind=kOutput, calls=%fused_computation.1 | convolution fusion | flops 45298483200 | bytes 30801920 | tf_op jit(solution)/shard_map/dot_general | solution.py:17
  255.4 7.7 %copy.94 = f32[1280,1152]{1,0:T(8,128)} copy(f32[1280,1152]{0,1:T(8,128)} %convolution_bitcast_fusion.1) | data formatting | bytes 11796480
  263.3 4.3 fusion.75
  267.6 9.3 %fusion.74 = (f32[2560,1,384]{0,2,1:T(8,128)}, f32[2560,1,384]{0,2,1:T(8,128)}, f32[2560,1,384]{0,2,1:T(8,128)}) fusion(f32[2560,3,384]{0,2,1:T(8,128)} %copy-done), kind=kLoop, calls=%fused_computation.100 | loop fusion | bytes 23592960 | tf_op jit(solution)/shard_map/slice | solution.py:72
  276.9 36.6 %reduce-scatter.7.cloned.1.call-done = f32[320,1152]{1,0:T(8,128)} async-done(((f32[2560,1152]{1,0:T(8,128)}), f32[320,1152]{1,0:T(8,128)}) %reduce-scatter.7.cloned.1.call-update) | async-done | bytes 1474576
  313.5 2.1 copy.93
  319.1 3.3 fusion.16
  323.5 3.3 fusion.18
  326.7 3.3 fusion.12
  331.9 3.2 fusion.14
  335.1 46.5 %reduce-scatter.9.cloned.1.call-done = f32[320,1152]{1,0:T(8,128)} async-done(((f32[1280,1152]{1,0:T(8,128)}), f32[320,1152]{1,0:T(8,128)}) %reduce-scatter.9.cloned.1.call-update) | async-done | bytes 1474576
  381.6 2.3 copy.95
  386.6 2.1 copy.100
  388.7 3.3 fusion.20
  393.1 3.2 fusion.49
  396.3 3.2 fusion.47
  402.5 2.2 pad_maximum_fusion
  407.0 137.7 %all-reduce.3.cloned.1.call-done = (f32[384,384]{1,0:T(8,128)}, f32[384,384]{1,0:T(8,128)}, f32[384,384]{1,0:T(8,128)}, f32[384,384]{1,0:T(8,128)}, f32[384,384]...) async-done(((f32[384,384]{1,0:T(8,128)}, f32[384,384]{1,0:T(8,128)}, f32[384,384]{1,0:T(8,128)}, f32[384,384]{1,0:T(8,128)}, f32[384,384]{1,0:T(8,128)}, ...) | async-done | bytes 4128784 | tf_op jit(solution)/shard_map/psum | solution.py:101
  546.3 2.5 fusion.7
  555.4 2.5 fusion.9
  (71 shorter events, 27.2 us)
Async XLA Ops:
  7.2 1.5 copy-start.16
  7.2 72.2 %all-gather.3.cloned.1.call-start = ((), (), s32[]{:S(2)}) async-start(), calls=%async_computation.2 | async-start | bytes 7372800 | tf_op jit(solution)/shard_map/all_gather | solution.py:54
  7.9 183.3 %all-gather.5.cloned.1.call-start = ((), (), s32[]{:S(2)}) async-start(), calls=%async_computation.3 | async-start | bytes 13271040 | tf_op jit(solution)/shard_map/all_gather | solution.py:55
  8.7 304.8 %reduce-scatter.7.cloned.1.call-start = ((), (), s32[]{:S(2)}) async-start(), calls=%async_computation.4 | async-start | bytes 13271040
  170.4 211.2 %reduce-scatter.9.cloned.1.call-start = ((), (), s32[]{:S(2)}) async-start(), calls=%async_computation.5 | async-start | bytes 7372800
  200.9 4.3 copy-start
  263.1 281.6 %all-reduce.3.cloned.1.call-start = ((), (), s32[]{:S(2)}) async-start(), calls=%async_computation.6 | async-start | bytes 8257536 | tf_op jit(solution)/shard_map/psum | solution.py:101
  317.8 4.5 copy-start.4
  319.1 3.3 copy-start.9
  331.1 0.8 copy-start.6
  385.2 6.8 %copy-start.1 = (f32[2,384,384]{2,1,0:T(8,128)S(1)}, f32[2,384,384]{2,1,0:T(8,128)}, u32[]{:S(2)}) copy-start(f32[2,384,384]{2,1,0:T(8,128)} %param.11) | copy-start | bytes 3538948
  388.7 3.3 copy-start.10
  400.4 2.1 copy-start.7
  404.7 1.1 copy-start.8
  544.7 1.5 copy-start.2
  544.7 1.6 copy-start.15
  544.7 4.2 copy-start.14
  546.1 2.7 copy-start.3
  546.1 2.7 copy-start.5
  548.8 1.3 copy-start.13
  550.1 1.3 copy-start.12
  551.5 1.6 copy-start.11
Sparse Core Ops, SparseCore 0:
  9.8 69.4 all-gather.2
  81.0 110.1 all-gather.4
  193.5 119.9 reduce-scatter.6
  316.4 65.2 reduce-scatter.8
  399.6 144.9 all-reduce.2
where the time goes:
time: 574 us; the launch traced here: 566 us
  waiting for transfers between devices  278 us (48%)
  matrix products  140 us (24%)
  local copies, waits for them, and re-layouts  105 us (18%)
  other arithmetic  26.1 us (5%)
  between operations  14.4 us (3%)
    psum x1, waiting for transfers between devices, per_device(): lax.psum(inner_product(upper_mine, inv_cols), ('row', 'col'))  138 us
    unnamed x7, waiting for transfers between devices  84.6 us
    dot_general x8, matrix products, inner_product(): lax.dot_general(left, right, (((0,), (0,)), ((), ())), precision=precise,...  72.9 us
    dot_general x9, matrix products, product(): jnp.dot(left, right, precision=precise, preferred_element_type=jnp.float32)  65.3 us
    all_gather x1, waiting for transfers between devices, per_device(): lax.all_gather(lower_anc, 'row', axis=2, tiled=True) * col_pattern  55.8 us
    unnamed x46, local copies, waits for them, and re-layouts  39.8 us
    reshape x2, local copies, waits for them, and re-layouts, tile_pattern(): return widened.reshape(blocks * BLK, SUPER, W)  24.2 us
  transfers between devices with their start and end apart: 5, of which 5 were waited for; matrix products, arithmetic and copies ran while one was open for 42% of the time, Pallas kernels for 0%

commit v1 on v0

--- a/solution.py
+++ b/solution.py
@@ -51,7 +51,7 @@
     upper_list = []
     cols_list = []
     rows_list = []
-    lower_full = lax.all_gather(lower_anc, "row", axis=2, tiled=True) * col_pattern
+    lower_full = jnp.concatenate(lax.all_gather(lower_anc, "row"), axis=2) * col_pattern
     upper_full = lax.all_gather(upper_anc, "col", axis=2, tiled=True) * row_pattern
     cols_all = lax.psum_scatter(
         row_term(anc_inverse, lower_full.reshape(cols_here, SUPER * W)),

time: 574 us -> 572 us (level)
  local copies, waits for them, and re-layouts: 105 us -> 114 us
  waiting for transfers between devices: 278 us -> 270 us
  matrix products: 140 us -> 147 us
    unnamed x7, waiting for transfers between devices: 84.6 us -> 59.4 us
    all_gather x1, waiting for transfers between devices: 55.8 us -> 70.5 us  [per_device(): lax.all_gather(lower_anc, 'row')]
    mul x1 -> x0, local copies, waits for them, and re-layouts: 7.76 us -> none  [per_device(): lax.all_gather(lower_anc, 'row', axis=2, tiled=True) * col_pattern]
    reshape x2 -> x3, local copies, waits for them, and re-layouts: 24.2 us -> 31.9 us  [tile_pattern(): return widened.reshape(blocks * BLK, SUPER, W)]
    broadcast_in_dim x2 -> x3, local copies, waits for them, and re-layouts: 10.2 us -> 14.8 us  [tile_pattern(): jnp.broadcast_to(window[:, None, :, :, None], (blocks, BLK, SUPER, W // B...]
    unnamed x46 -> x48, local copies, waits for them, and re-layouts: 39.8 us -> 40.5 us
  transfers between devices with their start and end apart: 5 -> 5, of which waited for: 5 -> 5; matrix products, arithmetic and copies ran while one was open for 42% -> 43% of each run, Pallas kernels for 0% -> 0%
where the time goes in v1:
time: 572 us; the launch traced here: 568 us
  waiting for transfers between devices  270 us (47%)
  matrix products  147 us (26%)
  local copies, waits for them, and re-layouts  114 us (20%)
  other arithmetic  22.1 us (4%)
  between operations  14.4 us (3%)
    psum x1, waiting for transfers between devices, per_device(): lax.psum(inner_product(upper_mine, inv_cols), ('row', 'col'))  137 us
    dot_general x8, matrix products, inner_product(): lax.dot_general(left, right, (((0,), (0,)), ((), ())), precision=precise,...  74.8 us
    all_gather x1, waiting for transfers between devices, per_device(): lax.all_gather(lower_anc, 'row')  70.5 us
    dot_general x9, matrix products, product(): jnp.dot(left, right, precision=precise, preferred_element_type=jnp.float32)  69.9 us
    unnamed x7, waiting for transfers between devices  59.4 us
    unnamed x48, local copies, waits for them, and re-layouts  40.5 us
    reshape x3, local copies, waits for them, and re-layouts, tile_pattern(): return widened.reshape(blocks * BLK, SUPER, W)  31.9 us
    broadcast_in_dim x3, local copies, waits for them, and re-layouts, tile_pattern(): jnp.broadcast_to(window[:, None, :, :, None], (blocks, BLK, SUPER, W // B...  14.8 us
  transfers between devices with their start and end apart: 5, of which 5 were waited for; matrix products, arithmetic and copies ran while one was open for 43% of the time, Pallas kernels for 0%

profile of v1, /device:TPU:0, one launch (start us, length us, event | category | flops | bytes accessed | tf_op | source)
XLA Modules:
  0.0 567.6 jit_solution(2790890702815255923)
XLA Ops:
  8.8 70.5 %all-gather.6.cloned.1.call-done = f32[5120,3,96]{0,2,1:T(8,128)} async-done(((f32[1280,3,96]{0,2,1:T(8,128)}), f32[5120,3,96]{0,2,1:T(8,128)}) %all-gather.6.cloned.1.call-update) | async-done | bytes 5898256 | tf_op jit(solution)/shard_map/all_gather | solution.py:54
  79.3 8.2 %reshape.61 = f32[4,1280,3,96]{1,0,3,2:T(4,128)} reshape(f32[5120,3,96]{0,2,1:T(8,128)} %all-gather.6.cloned.1.call-done) | data formatting | bytes 11796480 | tf_op jit(solution)/shard_map/all_gather | solution.py:54
  87.6 4.4 copy.78
  92.0 4.6 broadcast_in_dim.6.clone
  97.4 57.3 %convolution_bitcast_fusion = f32[2560,1152]{0,1:T(8,128)} fusion(f32[2560,1280]{1,0:T(8,128)} %param.7, f32[1280,1152]{0,1:T(8,128)S(1)} %bitcast.173, f32[144,8,10,128]{3,2,1,0:T(8,128)} %bitcast.176), kind=kOutput, calls=%fused_computation | convolution fusion | flops 45299957760 | bytes 36700160 | tf_op jit(solution)/shard_map/dot_general | solution.py:13
  154.7 13.6 %copy.105 = f32[2560,1152]{1,0:T(8,128)} copy(f32[2560,1152]{0,1:T(8,128)} %convolution_bitcast_fusion) | data formatting | bytes 23592960
  168.4 6.0 %broadcast_in_dim.7 = f32[20,128,3,3,128]{1,0,4,3,2:T(8,128)} broadcast(f32[20,3,3]{0,2,1:T(4,128)S(1)} %convert_bitcast_fusion), dimensions={0,2,3} | broadcast | bytes 11797200 | tf_op jit(solution)/shard_map/broadcast_in_dim | solution.py:31
  174.4 13.7 %reshape.56 = f32[2560,3,384]{0,2,1:T(8,128)} reshape(f32[20,128,3,3,128]{1,0,4,3,2:T(8,128)} %broadcast_in_dim.7) | data formatting | bytes 23592960 | tf_op jit(solution)/shard_map/reshape | solution.py:32
  188.1 3.0 all-gather.4.cloned.1.call-done
  191.2 9.7 %mul.35 = f32[2560,3,384]{0,2,1:T(8,128)S(1)} multiply(f32[2560,3,384]{0,2,1:T(8,128)} %all-gather.4.cloned.1.call-done, f32[2560,3,384]{0,2,1:T(8,128)} %reshape.56) | non-fusion elementwise | flops 2949120 | bytes 35389440 | tf_op jit(solution)/shard_map/mul | solution.py:55
  200.9 4.3 copy-done
  205.3 50.0 %convolution_bitcast_fusion.1 = f32[1280,1152]{0,1:T(8,128)} fusion(f32[2560,1152]{0,1:T(8,128)S(1)} %bitcast.172, f32[2560,1280]{1,0:T(8,128)} %param.7), kind=kOutput, calls=%fused_computation.1 | convolution fusion | flops 45298483200 | bytes 30801920 | tf_op jit(solution)/shard_map/dot_general | solution.py:17
  255.3 7.7 %copy.107 = f32[1280,1152]{1,0:T(8,128)} copy(f32[1280,1152]{0,1:T(8,128)} %convolution_bitcast_fusion.1) | data formatting | bytes 11796480
  263.1 4.2 broadcast_in_dim.6
  267.3 10.5 %reshape.60 = f32[1280,3,384]{2,0,1:T(8,128)} reshape(f32[10,128,3,3,128]{4,3,1,0,2:T(4,128)} %broadcast_in_dim.6) | data formatting | bytes 11796480 | tf_op jit(solution)/shard_map/reshape | solution.py:32
  277.8 7.7 %copy.89 = f32[1280,3,384]{0,2,1:T(8,128)} copy(f32[1280,3,384]{2,0,1:T(8,128)} %reshape.60) | data formatting | bytes 11796480 | tf_op jit(solution)/shard_map/reshape | solution.py:32
  285.5 5.2 bitcast_multiply_fusion.2
  292.9 9.2 %fusion.75 = (f32[2560,1,384]{0,2,1:T(8,128)}, f32[2560,1,384]{0,2,1:T(8,128)}, f32[2560,1,384]{0,2,1:T(8,128)}) fusion(f32[2560,3,384]{0,2,1:T(8,128)} %copy-done), kind=kLoop, calls=%fused_computation.103 | loop fusion | bytes 23592960 | tf_op jit(solution)/shard_map/slice | solution.py:72
  302.1 11.4 %reduce-scatter.7.cloned.1.call-done = f32[320,1152]{1,0:T(8,128)} async-done(((f32[2560,1152]{1,0:T(8,128)}), f32[320,1152]{1,0:T(8,128)}) %reduce-scatter.7.cloned.1.call-update) | async-done | bytes 1474576
  319.1 3.3 fusion.21
  323.5 3.2 fusion.23
  326.7 3.3 fusion.15
  331.9 3.2 fusion.17
  335.1 46.5 %reduce-scatter.9.cloned.1.call-done = f32[320,1152]{1,0:T(8,128)} async-done(((f32[1280,1152]{1,0:T(8,128)}), f32[320,1152]{1,0:T(8,128)}) %reduce-scatter.9.cloned.1.call-update) | async-done | bytes 1474576
  381.6 2.3 copy.108
  388.7 3.3 fusion.25
  393.1 4.2 fusion.19
  397.3 4.2 fusion.13
  404.5 2.3 pad_maximum_fusion
  409.1 137.5 %all-reduce.3.cloned.1.call-done = (f32[384,384]{1,0:T(8,128)}, f32[384,384]{1,0:T(8,128)}, f32[384,384]{1,0:T(8,128)}, f32[384,384]{1,0:T(8,128)}, f32[384,384]...) async-done(((f32[384,384]{1,0:T(8,128)}, f32[384,384]{1,0:T(8,128)}, f32[384,384]{1,0:T(8,128)}, f32[384,384]{1,0:T(8,128)}, f32[384,384]{1,0:T(8,128)}, ...) | async-done | bytes 4128784 | tf_op jit(solution)/shard_map/psum | solution.py:101
  548.2 2.6 fusion.8
  557.4 2.5 fusion.10
  (75 shorter events, 33.3 us)
Async XLA Ops:
  7.2 1.5 copy-start.17
  7.2 72.2 %all-gather.6.cloned.1.call-start = ((), (), s32[]{:S(2)}) async-start(), calls=%async_computation.3 | async-start | bytes 7372800 | tf_op jit(solution)/shard_map/all_gather | solution.py:54
  7.9 183.3 %all-gather.4.cloned.1.call-start = ((), (), s32[]{:S(2)}) async-start(), calls=%async_computation.2 | async-start | bytes 13271040 | tf_op jit(solution)/shard_map/all_gather | solution.py:55
  8.7 304.8 %reduce-scatter.7.cloned.1.call-start = ((), (), s32[]{:S(2)}) async-start(), calls=%async_computation.4 | async-start | bytes 13271040
  92.0 5.4 copy-start.1
  168.2 213.4 %reduce-scatter.9.cloned.1.call-start = ((), (), s32[]{:S(2)}) async-start(), calls=%async_computation.5 | async-start | bytes 7372800
  200.9 4.3 copy-start
  263.0 283.6 %all-reduce.3.cloned.1.call-start = ((), (), s32[]{:S(2)}) async-start(), calls=%async_computation.6 | async-start | bytes 8257536 | tf_op jit(solution)/shard_map/psum | solution.py:101
  317.8 4.5 copy-start.5
  319.0 3.3 copy-start.10
  331.1 0.8 copy-start.7
  385.2 6.8 %copy-start.2 = (f32[2,384,384]{2,1,0:T(8,128)S(1)}, f32[2,384,384]{2,1,0:T(8,128)}, u32[]{:S(2)}) copy-start(f32[2,384,384]{2,1,0:T(8,128)} %param.11) | copy-start | bytes 3538948
  388.7 3.3 copy-start.11
  402.4 2.1 copy-start.8
  404.5 3.4 copy-start.9
  546.6 1.5 copy-start.3
  546.6 1.6 copy-start.16
  546.6 4.2 copy-start.4
  546.6 4.2 copy-start.6
  546.6 4.2 copy-start.15
  550.8 1.3 copy-start.14
  552.1 1.6 copy-start.13
  552.1 2.9 copy-start.12
Sparse Core Ops, SparseCore 0:
  9.8 69.4 all-gather.5
  80.9 110.1 all-gather.3
  193.5 119.9 reduce-scatter.6
  316.4 65.2 reduce-scatter.8
  401.7 144.9 all-reduce.2
